TPU v7x, 256 devices: a whole 4x4x8 slice. The times are simulated.
256 devices in a mesh: row: 8 (over z), col: 16 (over y, x), smp: 2 (over core).
Axes of the slice: x: 4, y: 4, z: 8, core: 2. Of those that a mesh axis runs over, the one named last changes fastest.
Arguments:
- state: float32 [8, 2048, 512], P('smp', ('row', 'col')), may hold values from -6 to 6
- noise: float32 [2, 8, 2048, 512], P(None, 'smp', ('row', 'col')), may hold values from -6 to 6
- pair: bfloat16 [2048, 2048, 128], P('row', 'col'), may hold values from -10 to 10
- contacts: int32 [16, 6], replicated, may hold values from -1 to 15, as said below
- norm_gain: float32 [512], replicated, may hold values from 0.1 to 1.9
- w_qkv: bfloat16 [512, 1536], replicated, may hold values from -0.25 to 0.25
- w_out: bfloat16 [512, 512], replicated, may hold values from -0.25 to 0.25
- w_bias: bfloat16 [128, 32], replicated, may hold values from -1.5 to 1.5
Outputs:
- denoised: float32 [8, 2048, 512], P('smp', ('row', 'col'))
Inputs may be any that keep to these rules, and one draw needn't show every extreme that they name: `contacts`: row q lists distinct blocks, q itself first, then nearby blocks more often than far ones; its first counts are blocks and the remaining slots hold -1; some row uses all 6 slots.
All inputs are finite; a program needn't handle non-finite values.
Results may differ from a plain program's by a relative error of at most 0.012.
Values may be sent and summed in bfloat16 or wider, within the bound.
A program may use at most 128 MiB of HBM per device.

v0:
```python
import jax
import jax.numpy as jnp
from jax import lax
from jax.sharding import PartitionSpec as P

STEPS = 2


def from_root(block, axis, owner):
    block = jnp.where(lax.axis_index(axis) == owner, block, jnp.zeros_like(block))
    return lax.psum(block, axis)


def body(state, noise, pair, contacts, norm_gain, w_qkv, w_out, w_bias):
    samples_dev, rows_dev, width = state.shape
    heads = w_bias.shape[1]
    head_dim = width // heads
    row_span, blk = (pair.shape[0], pair.shape[1])
    per_row = row_span // blk
    half = row_span // lax.axis_size("smp")
    own_rows = lax.dynamic_slice_in_dim(pair, lax.axis_index("smp") * half, half, 0)
    part_bias = jnp.einsum(
        "ijc,ch->hij", own_rows, w_bias, preferred_element_type=jnp.float32
    ).astype(jnp.bfloat16)
    bias = lax.all_gather(part_bias, "smp", axis=1, tiled=True).astype(jnp.float32)
    col_index = lax.axis_index("col")
    row_index = lax.axis_index("row")
    listed = lax.dynamic_slice_in_dim(contacts, row_index * per_row, per_row, 0)
    matched = jnp.any(listed == col_index, axis=1)
    allowed = jnp.repeat(matched, blk, total_repeat_length=row_span)
    busy = jnp.any(matched)
    x = state
    for step in range(STEPS):
        mean = jnp.mean(x, axis=-1, keepdims=True)
        var = jnp.mean((x - mean) ** 2, axis=-1, keepdims=True)
        normed = ((x - mean) * lax.rsqrt(var + 1e-05) * norm_gain).astype(jnp.bfloat16)
        qkv = jnp.dot(normed, w_qkv, preferred_element_type=jnp.float32).astype(jnp.bfloat16)
        block_rows = lax.all_gather(qkv, "col", axis=1, tiled=True)
        offset = col_index % per_row * blk
        mine = lax.dynamic_slice_in_dim(block_rows[..., width:], offset, blk, 1)
        keyval = from_root(mine, "row", col_index // per_row)
        queries = block_rows[..., :width].reshape(samples_dev, row_span, heads, head_dim)
        keys = keyval[..., :width].reshape(samples_dev, blk, heads, head_dim)
        values = keyval[..., width:].reshape(samples_dev, blk, heads, head_dim)

        def attend(unused):
            scores = (
                jnp.einsum("srhd,skhd->hsrk", queries, keys, preferred_element_type=jnp.float32)
                * 0.25
                + bias[:, None]
            )
            m_raw = jnp.max(scores, axis=-1)
            m_blk = jnp.where(allowed[None, None, :], m_raw, jnp.float32(-1e30))
            probs = jnp.where(
                allowed[None, None, :, None], jnp.exp(scores - m_raw[..., None]), jnp.float32(0.0)
            )
            totals = jnp.sum(probs, axis=-1)
            outputs = jnp.einsum(
                "hsrk,skhd->srhd",
                probs.astype(jnp.bfloat16),
                values,
                preferred_element_type=jnp.float32,
            )
            return (
                m_blk.transpose(1, 2, 0),
                totals.transpose(1, 2, 0),
                outputs.reshape(samples_dev, row_span, width),
            )

        def skipped(unused):
            return (
                jnp.full((samples_dev, row_span, heads), -1e30, jnp.float32),
                jnp.zeros((samples_dev, row_span, heads), jnp.float32),
                jnp.zeros((samples_dev, row_span, width), jnp.float32),
            )

        m_blk, totals, outputs = lax.cond(busy, attend, skipped, 0)
        top = lax.pmax(m_blk.astype(jnp.bfloat16), "col").astype(m_blk.dtype)
        weight = jnp.exp(m_blk - top)
        scaled = (
            outputs.reshape(samples_dev, row_span, heads, head_dim) * weight[..., None]
        ).reshape(samples_dev, row_span, width)
        summed, acc = (
            lax.psum_scatter(totals * weight, "col", scatter_dimension=1, tiled=True),
            lax.psum_scatter(scaled, "col", scatter_dimension=1, tiled=True),
        )
        attn = (acc.reshape(samples_dev, rows_dev, heads, head_dim) / summed[..., None]).reshape(
            samples_dev, rows_dev, width
        )
        attn = attn.astype(jnp.bfloat16)
        out = jnp.dot(attn, w_out, preferred_element_type=jnp.float32)
        x = x + out + 0.5 * 0.5**step * noise[step]
    return x


def solution(mesh):
    in_specs = (
        P("smp", ("row", "col"), None),
        P(None, "smp", ("row", "col"), None),
        P("row", "col", None),
        P(),
        P(),
        P(),
        P(),
        P(),
    )
    out_specs = P("smp", ("row", "col"), None)
    return jax.shard_map(body, mesh=mesh, in_specs=in_specs, out_specs=out_specs, check_vma=False)
```

profile of v0, /device:TPU:32, one launch (start us, length us, event | category | flops | bytes accessed | tf_op | source)
XLA Modules:
  0.0 770.0 jit_solution(14538606355737976069)
XLA Ops:
  6.5 1.1 reduce_sum.54
  7.7 1.1 multiply_reduce_fusion.1
  8.7 2.0 convolution_convert_fusion.1
  10.8 0.0 all-gather.4.cloned.1.call-update
  10.8 0.0 all-gather.6.cloned.1.call-start
  10.8 4.8 fusion.23
  15.6 0.0 all-gather.6.cloned.1.call-update
  15.6 0.0 all-reduce.13.cloned.1.call-start
  15.7 50.6 %all-gather.4.cloned.1.call-done = bf16[4,256,1536]{2,1,0:T(8,128)(2,1)} async-done(((bf16[4,16,1536]{2,1,0:T(8,128)(2,1)}), bf16[4,256,1536]{2,1,0:T(8,128)(2,1)}) %all-gather.4.cloned.1.call-update) | async-done | bytes 3145744 | tf_op jit(solution)/shard_map/all_gather | solution.py:38
  66.3 1.6 slice-done
  67.9 1.2 dynamic-slice_select_fusion.1
  69.1 0.0 all-reduce.13.cloned.1.call-update
  69.2 0.0 all-reduce.15.cloned.1.call-start
  69.2 0.7 fusion.44
  70.6 0.6 fusion.49
  71.2 1.2 select_reduce_fusion
  72.5 10.4 %all-gather.6.cloned.1.call-done = bf16[32,256,128]{2,0,1:T(8,128)(2,1)} async-done(((bf16[32,128,128]{2,0,1:T(8,128)(2,1)}), bf16[32,256,128]{2,0,1:T(8,128)(2,1)}) %all-gather.6.cloned.1.call-update) | async-done | bytes 2097168 | tf_op jit(solution)/shard_map/all_gather | solution.py:25
  82.9 4.1 convert_element_type.54
  87.0 75.3 %all-reduce.13.cloned.1.call-done = bf16[4,128,1024]{2,1,0:T(8,128)(2,1)} async-done(((bf16[4,128,1024]{2,1,0:T(8,128)(2,1)}), bf16[4,128,1024]{2,1,0:T(8,128)(2,1)}) %all-reduce.13.cloned.1.call-update) | async-done | bytes 1048592 | tf_op jit(solution)/shard_map/psum | solution.py:11
  162.3 2.8 conditional.2
  162.3 0.7 broadcast.171.clone
  163.0 0.7 broadcast.172.clone
  163.6 1.5 broadcast.173
  165.1 1.5 convert_element_type.55
  166.7 0.0 all-reduce.15.cloned.1.call-update
  166.7 0.0 all-reduce.23.cloned.1.call-start
  166.7 117.8 %all-reduce.15.cloned.1.call-done = bf16[4,256,32]{1,2,0:T(8,128)(2,1)} async-done(((bf16[4,256,32]{1,2,0:T(8,128)(2,1)}), bf16[4,256,32]{1,2,0:T(8,128)(2,1)}) %all-reduce.15.cloned.1.call-update) | async-done | bytes 65552 | tf_op jit(solution)/shard_map/pmax | solution.py:78
  284.5 1.0 fusion.46
  285.5 3.2 bitcast_multiply_fusion.1
  288.7 3.1 copy.98
  291.8 1.1 copy.100
  292.9 0.0 all-reduce.23.cloned.1.call-update
  292.9 0.0 all-gather.8.cloned.1.call-start
  293.0 0.6 dynamic-slice.6
  294.2 101.5 %all-reduce.23.cloned.1.call-done = (f32[4,256,32]{2,0,1:T(4,128)}, f32[4,256,512]{2,0,1:T(4,128)}) async-done(((f32[4,256,32]{2,0,1:T(4,128)}, f32[4,256,512]{2,0,1:T(4,128)}), (f32[4,256,32]{2,0,1:T(4,128)}, f32[4,256,512]{2,0,1:T(4,128)})) %all-reduce.23.cloned.1.call-update) | async-done | bytes 2228240
  395.7 0.8 constant_dynamic-slice_fusion.2
  396.5 1.6 constant_dynamic-slice_fusion.3
  398.0 0.3 div.48
  398.4 0.6 div.49
  399.0 1.3 fusion.50
  400.3 0.2 multiply_reduce_fusion
  400.4 1.1 convolution_convert_fusion
  401.6 0.0 all-gather.8.cloned.1.call-update
  401.6 0.0 all-reduce.17.cloned.1.call-start
  401.6 52.2 %all-gather.8.cloned.1.call-done = bf16[4,256,1536]{2,1,0:T(8,128)(2,1)} async-done(((bf16[4,16,1536]{2,1,0:T(8,128)(2,1)}), bf16[4,256,1536]{2,1,0:T(8,128)(2,1)}) %all-gather.8.cloned.1.call-update) | async-done | bytes 3145744 | tf_op jit(solution)/shard_map/all_gather | solution.py:38
  453.8 1.6 slice-done.1
  455.4 1.2 dynamic-slice_select_fusion
  456.7 0.0 all-reduce.19.cloned.1.call-start
  456.7 74.6 %all-reduce.17.cloned.1.call-done = bf16[4,128,1024]{2,1,0:T(8,128)(2,1)} async-done(((bf16[4,128,1024]{2,1,0:T(8,128)(2,1)}), bf16[4,128,1024]{2,1,0:T(8,128)(2,1)}) %all-reduce.17.cloned.1.call-update) | async-done | bytes 1048592 | tf_op jit(solution)/shard_map/psum | solution.py:11
  531.3 1.5 conditional.3
  531.4 1.5 broadcast.177
  532.9 0.6 convert_element_type.60
  533.5 0.0 all-reduce.21.cloned.1.call-start
  533.6 114.5 %all-reduce.19.cloned.1.call-done = bf16[4,256,32]{1,2,0:T(8,128)(2,1)} async-done(((bf16[4,256,32]{1,2,0:T(8,128)(2,1)}), bf16[4,256,32]{1,2,0:T(8,128)(2,1)}) %all-reduce.19.cloned.1.call-update) | async-done | bytes 65552 | tf_op jit(solution)/shard_map/pmax | solution.py:78
  648.0 0.9 fusion.45
  648.9 3.1 bitcast_multiply_fusion
  652.1 3.2 copy.108
  655.3 1.0 copy.110
  656.3 102.8 %all-reduce.21.cloned.1.call-done = (f32[4,256,32]{2,0,1:T(4,128)}, f32[4,256,512]{2,0,1:T(4,128)}) async-done(((f32[4,256,32]{2,0,1:T(4,128)}, f32[4,256,512]{2,0,1:T(4,128)}), (f32[4,256,32]{2,0,1:T(4,128)}, f32[4,256,512]{2,0,1:T(4,128)})) %all-reduce.21.cloned.1.call-update) | async-done | bytes 2228240
  759.0 0.8 constant_dynamic-slice_fusion
  759.8 0.9 constant_dynamic-slice_fusion.1
  760.7 0.3 div.53
  761.1 0.6 div.54
  761.7 1.8 fusion.26
  (31 shorter events, 0.2 us)
Async XLA Ops:
  6.5 2.2 copy-start
  6.5 59.8 %all-gather.4.cloned.1.call-start = ((), (), s32[]{:S(2)}) async-start(), calls=%async_computation | async-start | bytes 3342336 | tf_op jit(solution)/shard_map/all_gather | solution.py:38
  10.8 72.1 %all-gather.6.cloned.1.call-start = ((), (), s32[]{:S(2)}) async-start(), calls=%async_computation.2 | async-start | bytes 3145728 | tf_op jit(solution)/shard_map/all_gather | solution.py:25
  15.6 53.6 %copy-start.9 = (s32[16,6]{0,1:T(8,128)S(1)}, s32[16,6]{0,1:T(8,128)}, u32[]{:S(2)}) copy-start(s32[16,6]{0,1:T(8,128)} %param.17) | copy-start | bytes 1156
  15.6 146.7 %all-reduce.13.cloned.1.call-start = ((), (), s32[]{:S(2)}) async-start(), calls=%async_computation.1 | async-start | bytes 2097152 | tf_op jit(solution)/shard_map/psum | solution.py:11
  66.3 1.6 slice-start
  69.2 215.3 %all-reduce.15.cloned.1.call-start = ((), (), s32[]{:S(2)}) async-start(), calls=%async_computation.3 | async-start | bytes 131072 | tf_op jit(solution)/shard_map/pmax | solution.py:78
  166.7 229.0 %all-reduce.23.cloned.1.call-start = ((), (), s32[]{:S(2)}) async-start(), calls=%async_computation.8 | async-start | bytes 5242880
  288.7 4.3 copy-start.10
  288.7 110.3 %copy-start.4 = (f32[4,16,512]{2,1,0:T(8,128)S(1)}, f32[4,16,512]{2,1,0:T(8,128)}, u32[]{:S(2)}) copy-start(f32[4,16,512]{2,1,0:T(8,128)} %param.14) | copy-start | bytes 393220
  288.7 110.3 %copy-start.5 = (bf16[512,512]{1,0:T(8,128)(2,1)S(1)}, bf16[512,512]{1,0:T(8,128)(2,1)}, u32[]{:S(2)}) copy-start(bf16[512,512]{1,0:T(8,128)(2,1)} %param.20) | copy-start | bytes 1572868
  291.8 108.6 %copy-start.8 = (f32[512]{0:T(512)S(1)}, f32[512]{0:T(512)}, u32[]{:S(2)}) copy-start(f32[512]{0:T(512)} %param.18) | copy-start | bytes 6148
  292.9 160.9 %all-gather.8.cloned.1.call-start = ((), (), s32[]{:S(2)}) async-start(), calls=%async_computation.4 | async-start | bytes 3342336 | tf_op jit(solution)/shard_map/all_gather | solution.py:38
  401.6 129.7 %all-reduce.17.cloned.1.call-start = ((), (), s32[]{:S(2)}) async-start(), calls=%async_computation.5 | async-start | bytes 2097152 | tf_op jit(solution)/shard_map/psum | solution.py:11
  453.8 1.6 slice-start.1
  456.7 191.4 %all-reduce.19.cloned.1.call-start = ((), (), s32[]{:S(2)}) async-start(), calls=%async_computation.6 | async-start | bytes 131072 | tf_op jit(solution)/shard_map/pmax | solution.py:78
  533.5 225.5 %all-reduce.21.cloned.1.call-start = ((), (), s32[]{:S(2)}) async-start(), calls=%async_computation.7 | async-start | bytes 5242880
  652.1 111.4 %copy-start.1 = (bf16[512,1536]{1,0:T(8,128)(2,1)S(1)}, bf16[512,1536]{1,0:T(8,128)(2,1)}, u32[]{:S(2)}) copy-start(bf16[512,1536]{1,0:T(8,128)(2,1)} %param.19) | copy-start | bytes 4718596
Sparse Core Ops, SparseCore 0:
  10.9 55.3 all-gather.3
  68.1 14.7 all-gather.5
  85.2 76.9 all-reduce.12
  166.8 117.6 all-reduce.14
  293.0 102.5 all-reduce.22
  401.7 52.0 all-gather.7
  456.8 74.5 all-reduce.16
  534.5 113.5 all-reduce.18
  656.4 102.5 all-reduce.20
where the time goes:
time: 771 us; the launch traced here: 770 us
  waiting for transfers between devices  700 us (91%)
  local copies, waits for them, and re-layouts  23.1 us (3%)
  other arithmetic  21.3 us (3%)
  between operations  14.7 us (2%)
  matrix products  10.9 us (1%)
    pmax x2, waiting for transfers between devices, body(): top = lax.pmax(m_blk.astype(jnp.bfloat16), 'col').astype(m_blk.dtype)  232 us
    unnamed x11, waiting for transfers between devices  204 us
    psum x2, waiting for transfers between devices, from_root(): return lax.psum(block, axis)  150 us
    all_gather x2, waiting for transfers between devices, body(): block_rows = lax.all_gather(qkv, 'col', axis=1, tiled=True)  103 us
  transfers between devices with their start and end apart: 9, of which 9 were waited for; matrix products, arithmetic and copies ran while one was open for 2% of the time, Pallas kernels for 0%

commit v1 on v0

v1 whole, which is shorter than its diff:
```python
import jax
import jax.numpy as jnp
from jax import lax
from jax.experimental import pallas as pl
from jax.experimental.pallas import tpu as pltpu
from jax.sharding import PartitionSpec as P


STEPS = 2
NZ, NC = 8, 16
SAMP, ROWS, DS = 4, 16, 512
HEADS, HD, CP = 32, 16, 128
BLK, KMAX = 128, 6
KEYS = KMAX * BLK
CHUNKS = 8
CH = BLK // CHUNKS
MESH = pl.DeviceIdType.MESH
BF, F32 = jnp.bfloat16, jnp.float32
NT = (((1,), (1,)), ((), ()))

OFFSETS = sorted(
    ((dy, dx) for dy in range(4) for dx in range(4) if (dy, dx) != (0, 0)),
    key=lambda o: -(min(o[0], 4 - o[0]) + min(o[1], 4 - o[1])),
)


def swap4(tiles, lane):
    a, b, c, d = tiles
    low = lane < 64
    a, c = jnp.where(low, a, pltpu.roll(c, 64, 1)), jnp.where(low, pltpu.roll(a, 64, 1), c)
    b, d = jnp.where(low, b, pltpu.roll(d, 64, 1)), jnp.where(low, pltpu.roll(b, 64, 1), d)
    even = (lane // 32) % 2 == 0
    a, b = jnp.where(even, a, pltpu.roll(b, 32, 1)), jnp.where(even, pltpu.roll(a, 96, 1), b)
    c, d = jnp.where(even, c, pltpu.roll(d, 32, 1)), jnp.where(even, pltpu.roll(c, 96, 1), d)
    return a, b, c, d


def kernel(
    state_ref, noise_ref, pair_ref, contacts_ref, gain_ref, wqkv_ref, wout_ref, wb_ref, out_ref,
    x_ref, pair_buf, stage, bias_send, bias_all, biasf, qkv_send, q_all, kv_first, kv_second, kcat, vcat,
    num, den, attn_send, attn_recv,
    pair_sem, bsend_sem, brecv_sem, fsend_sem, frecv_sem,
    kvsend_sem, kvrecv_sem, qsend_sem, qrecv_sem, local_sem,
    ring_send, ring_recv, asend_sem, arecv_sem,
):
    z, c, s = lax.axis_index("row"), lax.axis_index("col"), lax.axis_index("smp")
    y, x0 = c // 4, c % 4
    kv_all = (kv_first, kv_second)

    def col_at(o, sign):
        return ((y + sign * o[0] + 4) % 4) * 4 + (x0 + sign * o[1] + 4) % 4

    def drain(ref, sem):
        pltpu.make_async_copy(ref, ref, sem).wait()

    barrier = pltpu.get_barrier_semaphore()
    for o in OFFSETS:
        pl.semaphore_signal(barrier, inc=1, device_id={"col": col_at(o, 1)}, device_id_type=MESH)
    right, left = (z + 1) % NZ, (z + NZ - 1) % NZ
    pl.semaphore_signal(barrier, inc=1, device_id={"row": right}, device_id_type=MESH)
    pl.semaphore_signal(barrier, inc=1, device_id={"row": left}, device_id_type=MESH)
    pl.semaphore_signal(barrier, inc=1, device_id={"smp": 1 - s}, device_id_type=MESH)

    def pair_copy(ch):
        return pltpu.make_async_copy(
            pair_ref.at[pl.ds(s * BLK + ch * CH, CH)], pair_buf.at[pl.ds(ch * CH, CH)], pair_sem.at[ch]
        )

    for ch in range(CHUNKS):
        pair_copy(ch).start()

    lane = lax.broadcasted_iota(jnp.int32, (ROWS, 128), 1)

    def project(step):
        x = x_ref[...]
        mean = jnp.mean(x, axis=-1, keepdims=True)
        var = jnp.mean((x - mean) ** 2, axis=-1, keepdims=True)
        h = ((x - mean) * lax.rsqrt(var + 1e-05) * gain_ref[...]).astype(BF)
        for part in (1, 2, 0):
            y3 = jnp.dot(h, wqkv_ref[:, part * DS : (part + 1) * DS], preferred_element_type=F32)
            if part == 0:
                y3 = y3 * 0.25
            for t in range(4):
                tiles = [y3[k * ROWS : (k + 1) * ROWS, t * 128 : (t + 1) * 128] for k in range(SAMP)]
                for u, tile in enumerate(swap4(tiles, lane)):
                    qkv_send[step, 4 * t + u, part] = tile.astype(BF)

    def kv_slot(step, col):
        return kv_all[step].at[2 * z + col // 8, :, pl.ds(pl.multiple_of((col % 8) * ROWS, ROWS), ROWS), :]

    def rows_of(col):
        return pl.ds(pl.multiple_of(col * ROWS, ROWS), ROWS)

    def spread(step):
        half = c // 8
        for o in OFFSETS:
            to = col_at(o, 1)
            pltpu.make_async_remote_copy(
                src_ref=qkv_send.at[step, to, pl.ds(1, 2)],
                dst_ref=kv_slot(step, c),
                send_sem=kvsend_sem.at[step],
                recv_sem=kvrecv_sem.at[step, half],
                device_id={"col": to},
                device_id_type=MESH,
            ).start()
        pltpu.make_async_copy(
            qkv_send.at[step, c, pl.ds(1, 2)], kv_slot(step, c), kvrecv_sem.at[step, half]
        ).start()
        for o in OFFSETS:
            to = col_at(o, 1)
            pltpu.make_async_remote_copy(
                src_ref=qkv_send.at[step, to, 0],
                dst_ref=q_all.at[step, rows_of(c), :],
                send_sem=qsend_sem.at[step],
                recv_sem=qrecv_sem.at[step],
                device_id={"col": to},
                device_id_type=MESH,
            ).start()
        pltpu.make_async_copy(
            qkv_send.at[step, c, 0], q_all.at[step, rows_of(c), :], qrecv_sem.at[step]
        ).start()

    def ring_copy(step, way, t, j, plane):
        ref = kv_all[step].at[2 * plane + j // 2, j % 2]
        return pltpu.make_async_remote_copy(
            src_ref=ref,
            dst_ref=ref,
            send_sem=ring_send.at[step, way, t, j],
            recv_sem=ring_recv.at[step, way, t, j],
            device_id={"row": right if way == 0 else left},
            device_id_type=MESH,
        )

    def ring_plane(way, t):
        return (z - t + NZ) % NZ if way == 0 else (z + t) % NZ

    def ring_used(way, t, j):
        return t < 3 or (j < 2) == (way == 0)

    def ring(step):
        for t in range(4):
            for j in range(4):
                if t == 0 and j % 2 == 0:
                    drain(kv_all[step].at[2 * z + j // 2], kvrecv_sem.at[step, j // 2])
                for way in range(2):
                    if not ring_used(way, t, j):
                        continue
                    if t > 0:
                        ring_copy(step, way, t - 1, j, ring_plane(way, t)).wait_recv()
                    ring_copy(step, way, t, j, ring_plane(way, t)).start()

    def ring_finish(step):
        for way in range(2):
            for t in (2, 3):
                for j in range(4):
                    if ring_used(way, t, j) and not (t == 2 and ring_used(way, 3, j)):
                        ring_copy(step, way, t, j, ring_plane(way, t + 1)).wait_recv()

    def make_bias():
        wt = wb_ref[...].astype(F32).T.astype(BF)

        def chunk(ch, carry):
            pair_copy(ch).wait()
            for i in range(CH):
                stage[i * HEADS : (i + 1) * HEADS, :] = lax.dot_general(
                    wt, pair_buf[ch * CH + i], NT, preferred_element_type=F32
                )
            for h in range(HEADS):
                tile = stage[pl.ds(h, CH, stride=HEADS), :]
                bias_send[h // 2, h % 2, pl.ds(pl.multiple_of(ch * CH, CH), CH), :] = tile.astype(BF)
            return carry

        lax.fori_loop(0, CHUNKS, chunk, 0)

    def send_bias():
        for o in OFFSETS:
            to = col_at(o, 1)
            pltpu.make_async_remote_copy(
                src_ref=bias_send.at[to],
                dst_ref=bias_all.at[s, c],
                send_sem=bsend_sem,
                recv_sem=brecv_sem.at[c],
                device_id={"col": to},
                device_id_type=MESH,
            ).start()
        pltpu.make_async_copy(bias_send.at[c], bias_all.at[s, c], brecv_sem.at[c]).start()

    def pass_bias(col):
        drain(bias_all.at[s, col], brecv_sem.at[col])
        pltpu.make_async_remote_copy(
            src_ref=bias_all.at[s, col],
            dst_ref=bias_all.at[s, col],
            send_sem=fsend_sem,
            recv_sem=frecv_sem,
            device_id={"smp": 1 - s},
            device_id_type=MESH,
        ).start()

    def widen_bias():
        for qb in range(2):
            for slot in range(KMAX):
                kb = contacts_ref[2 * z + qb, slot]
                at = jnp.maximum(kb, 0)
                for hh in range(2):
                    tile = bias_all[qb, at, hh].astype(F32)
                    tile = jnp.where(kb >= 0, tile, F32(-1e30))
                    biasf[qb, hh * BLK : (hh + 1) * BLK, slot * BLK : (slot + 1) * BLK] = tile

    def attend(step):
        for qb in range(2):
            for slot in range(KMAX):
                at = jnp.maximum(contacts_ref[2 * z + qb, slot], 0)
                kcat[qb, slot * BLK : (slot + 1) * BLK, :] = kv_all[step][at, 0]
                vcat[qb, slot * BLK : (slot + 1) * BLK, 0:128] = kv_all[step][at, 1]
        wide = lax.broadcasted_iota(jnp.int32, (BLK, 128), 1) // HD

        def unit(it, carry):
            qb, sample = it // 4, it % 4
            q = q_all[step, pl.ds(pl.multiple_of(qb * BLK, BLK), BLK), :]
            picks = [wide == 2 * sample + hh for hh in range(2)]
            qs = jnp.concatenate([q * pick.astype(F32).astype(BF) for pick in picks], axis=0)
            scores = lax.dot_general(qs, kcat[qb], NT, preferred_element_type=F32) + biasf[qb]
            top = jnp.max(scores, axis=-1, keepdims=True)
            probs = jnp.exp(scores - top).astype(BF)
            both = jnp.dot(probs, vcat[qb], preferred_element_type=F32)
            at = pl.ds(pl.multiple_of(qb * BLK, BLK), BLK)
            n, d = num[at, :], den[at, :]
            for hh in range(2):
                part = both[hh * BLK : (hh + 1) * BLK]
                n = jnp.where(picks[hh], part[:, :128], n)
                d = jnp.where(picks[hh], part[:, 128:], d)
            num[at, :] = n
            den[at, :] = d
            return carry

        lax.fori_loop(0, 8, unit, 0)
        attn_send[step] = (num[...] / den[...]).astype(BF)

    def give_back(step):
        for o in OFFSETS:
            to = col_at(o, 1)
            pltpu.make_async_remote_copy(
                src_ref=attn_send.at[step, rows_of(to), :],
                dst_ref=attn_recv.at[step, c],
                send_sem=asend_sem.at[step],
                recv_sem=arecv_sem.at[step],
                device_id={"col": to},
                device_id_type=MESH,
            ).start()
        pltpu.make_async_copy(
            attn_send.at[step, rows_of(c), :], attn_recv.at[step, c], arecv_sem.at[step]
        ).start()
        drain(attn_recv.at[step], arecv_sem.at[step])

    def update(step):
        columns = []
        for t in range(4):
            tiles = [attn_recv[step, 4 * t + u].astype(F32) for u in range(4)]
            columns.append(swap4(tiles, lane))
        attn = jnp.concatenate(
            [jnp.concatenate([columns[t][k] for t in range(4)], axis=1) for k in range(SAMP)], axis=0
        ).astype(BF)
        out = jnp.dot(attn, wout_ref[...], preferred_element_type=F32)
        return x_ref[...] + out + 0.5 * 0.5**step * noise_ref[step]

    x_ref[...] = state_ref[...]
    vcat[:, :, 128:] = jnp.ones((2, KEYS, 128), BF)
    num[...] = jnp.zeros_like(num)
    den[...] = jnp.ones_like(den)
    project(0)
    pl.semaphore_wait(barrier, len(OFFSETS) + 3)
    for step in range(STEPS):
        if step:
            project(step)
        spread(step)
        if step == 0:
            make_bias()
            send_bias()
        ring(step)
        if step == 0:
            pass_bias(c)
            for o in reversed(OFFSETS):
                pass_bias(col_at(o, -1))
            drain(bias_all.at[1 - s], frecv_sem)
            widen_bias()
        ring_finish(step)
        drain(q_all.at[step], qrecv_sem.at[step])
        attend(step)
        give_back(step)
        x = update(step)
        if step < STEPS - 1:
            x_ref[...] = x
        else:
            out_ref[...] = x

    drain(bias_send.at[pl.ds(0, NC - 1)], bsend_sem)
    drain(bias_all.at[0], fsend_sem)
    for step in range(STEPS):
        drain(qkv_send.at[step, pl.ds(0, NC - 1), pl.ds(1, 2)], kvsend_sem.at[step])
        drain(q_all.at[step, pl.ds(0, (NC - 1) * ROWS), :], qsend_sem.at[step])
        drain(attn_send.at[step, pl.ds(0, (NC - 1) * ROWS), :], asend_sem.at[step])
        for way in range(2):
            for t in range(4):
                for j in range(4):
                    if ring_used(way, t, j):
                        ring_copy(step, way, t, j, ring_plane(way, t)).wait_send()


def body(state, noise, pair, contacts, norm_gain, w_qkv, w_out, w_bias):
    vmem = pl.BlockSpec(memory_space=pltpu.VMEM)
    dma = pltpu.SemaphoreType.DMA
    out = pl.pallas_call(
        kernel,
        out_shape=jax.ShapeDtypeStruct((SAMP * ROWS, DS), F32),
        in_specs=[
            vmem, vmem, pl.BlockSpec(memory_space=pltpu.HBM), pl.BlockSpec(memory_space=pltpu.SMEM),
            vmem, vmem, vmem, vmem,
        ],
        out_specs=vmem,
        scratch_shapes=[
            pltpu.VMEM((SAMP * ROWS, DS), F32),
            pltpu.VMEM((BLK, BLK, CP), BF),
            pltpu.VMEM((CH * HEADS, BLK), F32),
            pltpu.VMEM((NC, 2, BLK, BLK), BF),
            pltpu.VMEM((2, NC, 2, BLK, BLK), BF),
            pltpu.VMEM((2, 2 * BLK, KEYS), F32),
            pltpu.VMEM((STEPS, NC, 3, ROWS, 128), BF),
            pltpu.VMEM((STEPS, 2 * BLK, 128), BF),
            pltpu.VMEM((NC, 2, BLK, 128), BF),
            pltpu.VMEM((NC, 2, BLK, 128), BF),
            pltpu.VMEM((2, KEYS, 128), BF),
            pltpu.VMEM((2, KEYS, 256), BF),
            pltpu.VMEM((2 * BLK, 128), F32),
            pltpu.VMEM((2 * BLK, 128), F32),
            pltpu.VMEM((STEPS, 2 * BLK, 128), BF),
            pltpu.VMEM((STEPS, NC, ROWS, 128), BF),
            dma((CHUNKS,)),
            dma,
            dma((NC,)),
            dma,
            dma,
            dma((STEPS,)),
            dma((STEPS, 2)),
            dma((STEPS,)),
            dma((STEPS,)),
            dma,
            dma((STEPS, 2, 4, 4)),
            dma((STEPS, 2, 4, 4)),
            dma((STEPS,)),
            dma((STEPS,)),
        ],
        compiler_params=pltpu.CompilerParams(
            collective_id=0, has_side_effects=True, vmem_limit_bytes=56 * 1024 * 1024
        ),
        name="denoise",
    )(
        state.reshape(SAMP * ROWS, DS),
        noise.reshape(STEPS, SAMP * ROWS, DS),
        pair,
        contacts,
        norm_gain.reshape(1, DS),
        w_qkv,
        w_out,
        w_bias,
    )
    return out.reshape(SAMP, ROWS, DS)


def solution(mesh):
    in_specs = (
        P("smp", ("row", "col"), None),
        P(None, "smp", ("row", "col"), None),
        P("row", "col", None),
        P(),
        P(),
        P(),
        P(),
        P(),
    )
    out_specs = P("smp", ("row", "col"), None)
    return jax.shard_map(body, mesh=mesh, in_specs=in_specs, out_specs=out_specs, check_vma=False)
```

time: 771 us -> 79.4 us (0.10)
  waiting for transfers between devices: 700 us -> 0 us
  Pallas kernels: 0 us -> 74.8 us
  other arithmetic: 21.3 us -> 0 us
  local copies, waits for them, and re-layouts: 23.1 us -> 4.34 us
  between operations: 14.7 us -> 0.01 us
  matrix products: 10.9 us -> 0 us
    pmax x2 -> x0, waiting for transfers between devices: 232 us -> none  [body(): top = lax.pmax(m_blk.astype(jnp.bfloat16), 'col').astype(m_blk.dtype)]
    unnamed x11 -> x0, waiting for transfers between devices: 204 us -> none
    psum x2 -> x0, waiting for transfers between devices: 150 us -> none  [from_root(): return lax.psum(block, axis)]
    all_gather x3 -> x0, waiting for transfers between devices: 113 us -> none  [the longest x2 103 us: body(): block_rows = lax.all_gather(qkv, 'col', axis=1, tiled=True)]
    pallas_call x0 -> x1, Pallas kernels: none -> 74.8 us  [body(): pl.pallas_call(kernel, out_shape=jax.ShapeDtypeStruct((SAMP * ROWS, DS),...]
    dot_general x5 -> x0, matrix products: 10.9 us -> none  [the longest x1 4.75 us: body(): jnp.einsum('ijc,ch->hij', own_rows, w_bias, preferred_element_type=jnp.fl...]
    mul x4 -> x0, local copies, waits for them, and re-layouts: 8.39 us -> none  [the longest x2 6.33 us: body(): outputs.reshape(samples_dev, row_span, heads, head_dim) * weight[..., None]]
    mul x4 -> x0, other arithmetic: 8.21 us -> none  [the longest x2 6.34 us: body(): outputs.reshape(samples_dev, row_span, heads, head_dim) * weight[..., None]]
  transfers between devices with their start and end apart: 9 -> 0, of which waited for: 9 -> 0; matrix products, arithmetic and copies ran while one was open for 2% -> 0% of each run, Pallas kernels for 0% -> 0%
where the time goes in v1:
time: 79.4 us; the launch traced here: 79.2 us
  Pallas kernels  74.8 us (94%)
  local copies, waits for them, and re-layouts  4.34 us (5%)
    pallas_call x1, Pallas kernels, body(): pl.pallas_call(kernel, out_shape=jax.ShapeDtypeStruct((SAMP * ROWS, DS),...  74.8 us
    unnamed x3, local copies, waits for them, and re-layouts  4.34 us

profile of v1, /device:TPU:32, one launch (start us, length us, event | category | flops | bytes accessed | tf_op | source)
XLA Modules:
  0.0 79.2 jit_solution(7573040300548654715)
XLA Ops:
  0.0 1.4 %copy.9.contacts_ref = s32[16,6]{1,0:T(8,128)} copy(s32[16,6]{0,1:T(8,128)} %param.11) | data formatting | bytes 768 | tf_op args[3]
  1.4 1.4 %copy.10.wb_ref = bf16[128,32]{1,0:T(8,128)(2,1)} copy(bf16[128,32]{0,1:T(8,128)(2,1)} %param.15) | data formatting | bytes 16384 | tf_op args[7]
  2.8 74.8 %denoise.1 = f32[64,512]{1,0:T(8,128)} custom-call(f32[64,512]{1,0:T(8,128)} %bitcast.6, f32[2,64,512]{2,1,0:T(8,128)} %bitcast.5, bf16[256,128,128]{2,1,0:T(8,128)(2,1)} %pair_ref.1, s32[16,6]{1,0:T(8,128)} %copy.9.contacts_ref, f32[1,512]{1,0:T(1,128)} %bitcast.7, bf16[512,1536]{1,0:T(8,128)(2,1)} %wqkv_ref.1, bf16[512,512]{1,0:T(8,128)(2,1)} %wout_ref.1, ...), custom_call_target="tpu_custom_call" | custom-call | tf_op jit(solution)/shard_map/denoise/pallas_call | solution.py:312
  77.6 1.6 %copy.12 = f32[4,16,512]{2,1,0:T(8,128)} copy(f32[4,16,512]{2,1,0:T(8,128)} %bitcast.4) | data formatting | bytes 262144

commit v2 on v1

v2 whole, which is shorter than its diff:
```python
import jax
import jax.numpy as jnp
from jax import lax
from jax.experimental import pallas as pl
from jax.experimental.pallas import tpu as pltpu
from jax.sharding import PartitionSpec as P


STEPS = 2
NZ, NC = 8, 16
SAMP, ROWS, DS = 4, 16, 512
HEADS, HD, CP = 32, 16, 128
BLK, KMAX = 128, 6
KEYS = KMAX * BLK
CHUNKS = 8
CH = BLK // CHUNKS
PIECES = 1
J = 1
STRIP = 64
MESH = pl.DeviceIdType.MESH
BF, F32 = jnp.bfloat16, jnp.float32
NT = (((1,), (1,)), ((), ()))

OFFSETS = sorted(
    ((dy, dx) for dy in range(4) for dx in range(4) if (dy, dx) != (0, 0)),
    key=lambda o: -(min(o[0], 4 - o[0]) + min(o[1], 4 - o[1])),
)


def swap4(tiles, lane):
    a, b, c, d = tiles
    low = lane < 64
    a, c = jnp.where(low, a, pltpu.roll(c, 64, 1)), jnp.where(low, pltpu.roll(a, 64, 1), c)
    b, d = jnp.where(low, b, pltpu.roll(d, 64, 1)), jnp.where(low, pltpu.roll(b, 64, 1), d)
    even = (lane // 32) % 2 == 0
    a, b = jnp.where(even, a, pltpu.roll(b, 32, 1)), jnp.where(even, pltpu.roll(a, 96, 1), b)
    c, d = jnp.where(even, c, pltpu.roll(d, 32, 1)), jnp.where(even, pltpu.roll(c, 96, 1), d)
    return a, b, c, d


def kernel(
    state_ref, noise_ref, pair_ref, contacts_ref, gain_ref, wqkv_ref, wout_ref, wb_ref, out_ref,
    x_ref, pair_buf, stage, bias_send, bias_all, qkv_send, qkv_recv, k_first, k_second, v_first, v_second,
    kcat, vcat, scores, probs, num, den, attn_send, attn_recv,
    pair_sem, bsend_sem, brecv_sem, fsend_sem, frecv_sem,
    ssend_sem, srecv_sem,
    ring_send, ring_recv, asend_sem, arecv_sem,
):
    z, c, s = lax.axis_index("row"), lax.axis_index("col"), lax.axis_index("smp")
    y, x0 = c // 4, c % 4
    kv_all = ((k_first, v_first), (k_second, v_second))

    def col_at(o, sign):
        return ((y + sign * o[0] + 4) % 4) * 4 + (x0 + sign * o[1] + 4) % 4

    def drain(ref, sem):
        pltpu.make_async_copy(ref, ref, sem).wait()

    barrier = pltpu.get_barrier_semaphore()
    for o in OFFSETS:
        pl.semaphore_signal(barrier, inc=1, device_id={"col": col_at(o, 1)}, device_id_type=MESH)
    right, left = (z + 1) % NZ, (z + NZ - 1) % NZ
    pl.semaphore_signal(barrier, inc=1, device_id={"row": right}, device_id_type=MESH)
    pl.semaphore_signal(barrier, inc=1, device_id={"row": left}, device_id_type=MESH)
    pl.semaphore_signal(barrier, inc=1, device_id={"smp": 1 - s}, device_id_type=MESH)

    def pair_copy(ch):
        return pltpu.make_async_copy(
            pair_ref.at[pl.ds(s * BLK + ch * CH, CH)], pair_buf.at[pl.ds(ch * CH, CH)], pair_sem.at[ch]
        )

    for ch in range(CHUNKS):
        pair_copy(ch).start()

    lane = lax.broadcasted_iota(jnp.int32, (ROWS, 128), 1)

    def project(step):
        x = x_ref[...]
        mean = jnp.mean(x, axis=-1, keepdims=True)
        var = jnp.mean((x - mean) ** 2, axis=-1, keepdims=True)
        h = ((x - mean) * lax.rsqrt(var + 1e-05) * gain_ref[...]).astype(BF)
        for part in (1, 2, 0):
            y3 = jnp.dot(h, wqkv_ref[:, part * DS : (part + 1) * DS], preferred_element_type=F32)
            if part == 0:
                y3 = y3 * 0.25
            for t in range(4):
                tiles = [y3[k * ROWS : (k + 1) * ROWS, t * 128 : (t + 1) * 128] for k in range(SAMP)]
                for u, tile in enumerate(swap4(tiles, lane)):
                    qkv_send[step, 4 * t + u, part] = tile.astype(BF)

    def rows_of(col):
        return pl.ds(pl.multiple_of(col * ROWS, ROWS), ROWS)

    def spread(step):
        dst, sem = qkv_recv.at[step, :, c // 8, rows_of(c % 8), :], srecv_sem.at[step]
        for o in OFFSETS:
            to = col_at(o, 1)
            pltpu.make_async_remote_copy(
                src_ref=qkv_send.at[step, to],
                dst_ref=dst,
                send_sem=ssend_sem.at[step],
                recv_sem=sem,
                device_id={"col": to},
                device_id_type=MESH,
            ).start()
        pltpu.make_async_copy(qkv_send.at[step, c], dst, sem).start()

    def ring_copy(step, kv, way, t, j, plane):
        dst = kv_all[step][kv].at[pl.ds(2 * plane + j * (2 // J), 2 // J)]
        src = qkv_recv.at[step, kv + 1, pl.ds(j * (2 // J), 2 // J)] if t == 0 else dst
        return pltpu.make_async_remote_copy(
            src_ref=src,
            dst_ref=dst,
            send_sem=ring_send.at[step, kv, way, t, j],
            recv_sem=ring_recv.at[step, kv, way, t, j],
            device_id={"row": right if way == 0 else left},
            device_id_type=MESH,
        )

    def ring_plane(way, t):
        return (z - t + NZ) % NZ if way == 0 else (z + t) % NZ

    def ring_used(kv, way, t, j):
        return t < 3 or (way == kv if J == 1 else (j < J // 2) == (way == 0))

    def ring_turn(step, kv, t):
        for j in range(J):
            for way in range(2):
                if not ring_used(kv, way, t, j):
                    continue
                if t > 0:
                    ring_copy(step, kv, way, t - 1, j, ring_plane(way, t)).wait_recv()
                ring_copy(step, kv, way, t, j, ring_plane(way, t)).start()

    def ring_finish(step, kv):
        for t in (2, 3):
            for way in range(2):
                for j in range(J):
                    if ring_used(kv, way, t, j) and not (t == 2 and ring_used(kv, way, 3, j)):
                        ring_copy(step, kv, way, t, j, ring_plane(way, t + 1)).wait_recv()

    def make_bias():
        wt = wb_ref[...]

        def chunk(ch, carry):
            pair_copy(ch).wait()
            for i in range(CH):
                stage[i * HEADS : (i + 1) * HEADS, :] = lax.dot_general(
                    wt, pair_buf[ch * CH + i], NT, preferred_element_type=F32
                )
            for h in range(HEADS):
                tile = stage[pl.ds(h, CH, stride=HEADS), :]
                bias_send[h // 2, h % 2, pl.ds(pl.multiple_of(ch * CH, CH), CH), :] = tile.astype(BF)
            return carry

        for g in range(PIECES):
            lax.fori_loop(g * CHUNKS // PIECES, (g + 1) * CHUNKS // PIECES, chunk, 0)
            part = pl.ds(g * BLK // PIECES, BLK // PIECES)
            for o in OFFSETS:
                to = col_at(o, 1)
                pltpu.make_async_remote_copy(
                    src_ref=bias_send.at[to, :, part, :],
                    dst_ref=bias_all.at[s, c, :, part, :],
                    send_sem=bsend_sem,
                    recv_sem=brecv_sem.at[c],
                    device_id={"col": to},
                    device_id_type=MESH,
                ).start()
        pltpu.make_async_copy(bias_send.at[c], bias_all.at[s, c], brecv_sem.at[c]).start()

    def pass_bias(col):
        drain(bias_all.at[s, col], brecv_sem.at[col])
        pltpu.make_async_remote_copy(
            src_ref=bias_all.at[s, col],
            dst_ref=bias_all.at[s, col],
            send_sem=fsend_sem,
            recv_sem=frecv_sem,
            device_id={"smp": 1 - s},
            device_id_type=MESH,
        ).start()

    def slot_of(qb, slot):
        return contacts_ref[slot, 2 * z + qb]

    def place_bias():
        for qb in range(2):
            for slot in range(KMAX):
                kb = slot_of(qb, slot)
                at = jnp.maximum(kb, 0)
                for hh in range(2):
                    tile = jnp.where(kb >= 0, bias_all[qb, at, hh].astype(F32).T, F32(-1e30))
                    kcat[qb, hh, slot * BLK : (slot + 1) * BLK, 128:] = tile.astype(BF)

    def block_of(step, kv, kb):
        return kv_all[step][kv][jnp.maximum(kb, 0)]

    def place_keys(step):
        for qb in range(2):
            for slot in range(KMAX):
                tile = block_of(step, 0, slot_of(qb, slot))
                for hh in range(2):
                    kcat[qb, hh, slot * BLK : (slot + 1) * BLK, :128] = tile

    def place_values(step):
        for qb in range(2):
            for slot in range(KMAX):
                tile = block_of(step, 1, slot_of(qb, slot))
                vcat[qb, slot * BLK : (slot + 1) * BLK, :128] = tile

    wide = lax.broadcasted_iota(jnp.int32, (BLK, 128), 1)
    diagonal = (lax.broadcasted_iota(jnp.int32, (BLK, 128), 0) == wide).astype(F32).astype(BF)

    def soften(step, lo, hi):
        def unit(it, carry):
            qb, hh = it // 2, it % 2
            q = qkv_recv[step, 0, qb]
            rows = []
            for k in range(SAMP):
                pick = (wide // HD == 2 * k + hh).astype(F32).astype(BF)
                rows.append(jnp.concatenate([q * pick, diagonal], axis=1))
            qs = jnp.concatenate(rows, axis=0)
            for n in range(KEYS // 256):
                cols = slice(n * 256, (n + 1) * 256)
                scores[:, cols] = lax.dot_general(qs, kcat[qb, hh, cols, :], NT, preferred_element_type=F32)
            for k in range(0, SAMP * BLK, STRIP):
                strip = scores[k : k + STRIP, :]
                top = jnp.max(strip, axis=-1, keepdims=True)
                probs[it, k : k + STRIP, :] = jnp.exp(strip - top).astype(BF)
            return carry

        lax.fori_loop(lo, hi, unit, 0)

    def mix(step):
        def unit(it, carry):
            qb, hh = it // 2, it % 2
            both = jnp.dot(probs[it], vcat[qb], preferred_element_type=F32)
            at = pl.ds(pl.multiple_of(qb * BLK, BLK), BLK)
            n, d = num[at, :], den[at, :]
            for k in range(SAMP):
                pick = wide // HD == 2 * k + hh
                part = both[k * BLK : (k + 1) * BLK]
                n = jnp.where(pick, part[:, :128], n)
                d = jnp.where(pick, part[:, 128:], d)
            num[at, :] = n
            den[at, :] = d
            return carry

        lax.fori_loop(0, 4, unit, 0)
        attn_send[step] = (num[...] / den[...]).astype(BF)

    def give_back(step):
        for o in OFFSETS:
            to = col_at(o, 1)
            pltpu.make_async_remote_copy(
                src_ref=attn_send.at[step, rows_of(to), :],
                dst_ref=attn_recv.at[step, c],
                send_sem=asend_sem.at[step],
                recv_sem=arecv_sem.at[step],
                device_id={"col": to},
                device_id_type=MESH,
            ).start()
        pltpu.make_async_copy(
            attn_send.at[step, rows_of(c), :], attn_recv.at[step, c], arecv_sem.at[step]
        ).start()
        drain(attn_recv.at[step], arecv_sem.at[step])

    def update(step):
        columns = []
        for t in range(4):
            tiles = [attn_recv[step, 4 * t + u].astype(F32) for u in range(4)]
            columns.append(swap4(tiles, lane))
        attn = jnp.concatenate(
            [jnp.concatenate([columns[t][k] for t in range(4)], axis=1) for k in range(SAMP)], axis=0
        ).astype(BF)
        out = jnp.dot(attn, wout_ref[...], preferred_element_type=F32)
        return x_ref[...] + out + 0.5 * 0.5**step * noise_ref[step]

    x_ref[...] = state_ref[...]
    vcat[:, :, 128:] = jnp.ones((2, KEYS, 128), BF)
    num[...] = jnp.zeros_like(num)
    den[...] = jnp.ones_like(den)
    project(0)
    pl.semaphore_wait(barrier, len(OFFSETS) + 3)
    for step in range(STEPS):
        if step:
            project(step)
        spread(step)
        if step == 0:
            make_bias()
        drain(qkv_recv.at[step], srecv_sem.at[step])
        ring_turn(step, 0, 0)
        ring_turn(step, 1, 0)
        for kv in range(2):
            kv_all[step][kv][pl.ds(2 * z, 2)] = qkv_recv[step, kv + 1]
        for t in range(1, 4):
            ring_turn(step, 0, t)
            ring_turn(step, 1, t)
        ring_finish(step, 0)
        place_keys(step)
        if step == 0:
            pass_bias(c)
            for o in reversed(OFFSETS):
                pass_bias(col_at(o, -1))
            drain(bias_all.at[1 - s], frecv_sem)
            place_bias()
        soften(step, 0, 4)
        ring_finish(step, 1)
        place_values(step)
        mix(step)
        give_back(step)
        x = update(step)
        if step < STEPS - 1:
            x_ref[...] = x
        else:
            out_ref[...] = x

    drain(bias_send.at[pl.ds(0, NC - 1)], bsend_sem)
    drain(bias_all.at[0], fsend_sem)
    for step in range(STEPS):
        drain(qkv_send.at[step, pl.ds(0, NC - 1)], ssend_sem.at[step])
        drain(attn_send.at[step, pl.ds(0, (NC - 1) * ROWS), :], asend_sem.at[step])
        for kv in range(2):
            for way in range(2):
                for t in range(4):
                    for j in range(J):
                        if ring_used(kv, way, t, j):
                            ring_copy(step, kv, way, t, j, ring_plane(way, t)).wait_send()


def body(state, noise, pair, contacts, norm_gain, w_qkv, w_out, w_bias):
    vmem = pl.BlockSpec(memory_space=pltpu.VMEM)
    dma = pltpu.SemaphoreType.DMA
    out = pl.pallas_call(
        kernel,
        out_shape=jax.ShapeDtypeStruct((SAMP * ROWS, DS), F32),
        in_specs=[
            vmem, vmem, pl.BlockSpec(memory_space=pltpu.HBM), pl.BlockSpec(memory_space=pltpu.SMEM),
            vmem, vmem, vmem, vmem,
        ],
        out_specs=vmem,
        scratch_shapes=[
            pltpu.VMEM((SAMP * ROWS, DS), F32),
            pltpu.VMEM((BLK, BLK, CP), BF),
            pltpu.VMEM((CH * HEADS, BLK), F32),
            pltpu.VMEM((NC, 2, BLK, BLK), BF),
            pltpu.VMEM((2, NC, 2, BLK, BLK), BF),
            pltpu.VMEM((STEPS, NC, 3, ROWS, 128), BF),
            pltpu.VMEM((STEPS, 3, 2, BLK, 128), BF),
            pltpu.VMEM((NC, BLK, 128), BF),
            pltpu.VMEM((NC, BLK, 128), BF),
            pltpu.VMEM((NC, BLK, 128), BF),
            pltpu.VMEM((NC, BLK, 128), BF),
            pltpu.VMEM((2, 2, KEYS, 256), BF),
            pltpu.VMEM((2, KEYS, 256), BF),
            pltpu.VMEM((SAMP * BLK, KEYS), F32),
            pltpu.VMEM((4, SAMP * BLK, KEYS), BF),
            pltpu.VMEM((2 * BLK, 128), F32),
            pltpu.VMEM((2 * BLK, 128), F32),
            pltpu.VMEM((STEPS, 2 * BLK, 128), BF),
            pltpu.VMEM((STEPS, NC, ROWS, 128), BF),
            dma((CHUNKS,)),
            dma,
            dma((NC,)),
            dma,
            dma,
            dma((STEPS,)),
            dma((STEPS,)),
            dma((STEPS, 2, 2, 4, J)),
            dma((STEPS, 2, 2, 4, J)),
            dma((STEPS,)),
            dma((STEPS,)),
        ],
        compiler_params=pltpu.CompilerParams(
            collective_id=0, has_side_effects=True, vmem_limit_bytes=56 * 1024 * 1024
        ),
        name="denoise",
    )(
        state.reshape(SAMP * ROWS, DS),
        noise.reshape(STEPS, SAMP * ROWS, DS),
        pair,
        contacts.T,
        norm_gain.reshape(1, DS),
        w_qkv,
        w_out,
        w_bias.T,
    )
    return out.reshape(SAMP, ROWS, DS)


def solution(mesh):
    in_specs = (
        P("smp", ("row", "col"), None),
        P(None, "smp", ("row", "col"), None),
        P("row", "col", None),
        P(),
        P(),
        P(),
        P(),
        P(),
    )
    out_specs = P("smp", ("row", "col"), None)
    return jax.shard_map(body, mesh=mesh, in_specs=in_specs, out_specs=out_specs, check_vma=False)
```

time: 79.4 us -> 72.4 us (0.912)
  Pallas kernels: 74.8 us -> 70.7 us
  local copies, waits for them, and re-layouts: 4.34 us -> 1.57 us
    pallas_call x1, Pallas kernels: 74.8 us -> 70.7 us  [body(): pl.pallas_call(kernel, out_shape=jax.ShapeDtypeStruct((SAMP * ROWS, DS),...]
    unnamed x3 -> x1, local copies, waits for them, and re-layouts: 4.34 us -> 1.57 us
where the time goes in v2:
time: 72.4 us; the launch traced here: 72.3 us
  Pallas kernels  70.7 us (98%)
  local copies, waits for them, and re-layouts  1.57 us (2%)
    pallas_call x1, Pallas kernels, body(): pl.pallas_call(kernel, out_shape=jax.ShapeDtypeStruct((SAMP * ROWS, DS),...  70.7 us
    unnamed x1, local copies, waits for them, and re-layouts  1.57 us

profile of v2, /device:TPU:32, one launch (start us, length us, event | category | flops | bytes accessed | tf_op | source)
XLA Modules:
  0.0 72.3 jit_solution(7599617280805506837)
XLA Ops:
  0.0 70.7 %denoise.1 = f32[64,512]{1,0:T(8,128)} custom-call(f32[64,512]{1,0:T(8,128)} %bitcast.8, f32[2,64,512]{2,1,0:T(8,128)} %bitcast.7, bf16[256,128,128]{2,1,0:T(8,128)(2,1)} %pair_ref.1, s32[6,16]{1,0:T(8,128)} %bitcast.10, f32[1,512]{1,0:T(1,128)} %bitcast.11, bf16[512,1536]{1,0:T(8,128)(2,1)} %wqkv_ref.1, bf16[512,512]{1,0:T(8,128)(2,1)} %wout_ref.1, ...), custom_call_target="tpu_custom_call" | custom-call | tf_op jit(solution)/shard_map/denoise/pallas_call | solution.py:333
  70.7 1.6 %copy.10 = f32[4,16,512]{2,1,0:T(8,128)} copy(f32[4,16,512]{2,1,0:T(8,128)} %bitcast.6) | data formatting | bytes 262144

commit v3 on v2

--- a/solution.py
+++ b/solution.py
@@ -15,7 +15,12 @@
 CHUNKS = 8
 CH = BLK // CHUNKS
 PIECES = 1
-J = 1
+EARLY = 3
+FIRST = tuple((0, w, j) for j in range(2) for w in (1, -1))
+LATER = tuple((kv, o * w, w, j) for o in (1, 2) for kv in range(2) for j in range(2) for w in (1, -1)) + tuple(
+    (kv, 3 * w, w, j) for kv in range(2) for w, j in ((1, 0), (-1, 1))
+)
+COMES = (1, -1, 2, -2, 3, -3, 4)
 STRIP = 64
 MESH = pl.DeviceIdType.MESH
 BF, F32 = jnp.bfloat16, jnp.float32
@@ -39,11 +44,12 @@
 
 
 def kernel(
-    state_ref, noise_ref, pair_ref, contacts_ref, gain_ref, wqkv_ref, wout_ref, wb_ref, out_ref,
+    state_hbm, noise_hbm, pair_ref, contacts_ref, gain_ref, wqkv_hbm, wout_hbm, wb_ref, out_ref,
+    noise_ref, wqkv_ref, wout_ref, load_sem,
     x_ref, pair_buf, stage, bias_send, bias_all, qkv_send, qkv_recv, k_first, k_second, v_first, v_second,
     kcat, vcat, scores, probs, num, den, attn_send, attn_recv,
     pair_sem, bsend_sem, brecv_sem, fsend_sem, frecv_sem,
-    ssend_sem, srecv_sem,
+    ssend_sem, srecv_sem, krecv_sem,
     ring_send, ring_recv, asend_sem, arecv_sem,
 ):
     z, c, s = lax.axis_index("row"), lax.axis_index("col"), lax.axis_index("smp")
@@ -56,12 +62,12 @@
     def drain(ref, sem):
         pltpu.make_async_copy(ref, ref, sem).wait()
 
+    waited = set()
     barrier = pltpu.get_barrier_semaphore()
     for o in OFFSETS:
         pl.semaphore_signal(barrier, inc=1, device_id={"col": col_at(o, 1)}, device_id_type=MESH)
-    right, left = (z + 1) % NZ, (z + NZ - 1) % NZ
-    pl.semaphore_signal(barrier, inc=1, device_id={"row": right}, device_id_type=MESH)
-    pl.semaphore_signal(barrier, inc=1, device_id={"row": left}, device_id_type=MESH)
+    for d in range(1, NZ):
+        pl.semaphore_signal(barrier, inc=1, device_id={"row": (z + d) % NZ}, device_id_type=MESH)
     pl.semaphore_signal(barrier, inc=1, device_id={"smp": 1 - s}, device_id_type=MESH)
 
     def pair_copy(ch):
@@ -69,8 +75,20 @@
             pair_ref.at[pl.ds(s * BLK + ch * CH, CH)], pair_buf.at[pl.ds(ch * CH, CH)], pair_sem.at[ch]
         )
 
+
+    loads = [
+        pltpu.make_async_copy(src, dst, load_sem.at[k])
+        for k, (src, dst) in enumerate(
+            ((state_hbm, x_ref), (wqkv_hbm, wqkv_ref), (wout_hbm, wout_ref), (noise_hbm, noise_ref))
+        )
+    ]
+
+    for load in loads[:2]:
+        load.start()
     for ch in range(CHUNKS):
         pair_copy(ch).start()
+    for load in loads[2:]:
+        load.start()
 
     lane = lax.broadcasted_iota(jnp.int32, (ROWS, 128), 1)
 
@@ -86,78 +104,73 @@
             for t in range(4):
                 tiles = [y3[k * ROWS : (k + 1) * ROWS, t * 128 : (t + 1) * 128] for k in range(SAMP)]
                 for u, tile in enumerate(swap4(tiles, lane)):
-                    qkv_send[step, 4 * t + u, part] = tile.astype(BF)
+                    qkv_send[step, 4 * t + u, (part + 2) % 3] = tile.astype(BF)
+            if part == 1:
+                if step == 0:
+                    lax.fori_loop(0, EARLY, chunk, 0)
+                    pl.semaphore_wait(barrier, len(OFFSETS) + NZ)
+                spread(step, 0, 1, krecv_sem.at[step])
+        spread(step, 1, 2, srecv_sem.at[step])
 
     def rows_of(col):
         return pl.ds(pl.multiple_of(col * ROWS, ROWS), ROWS)
 
-    def spread(step):
-        dst, sem = qkv_recv.at[step, :, c // 8, rows_of(c % 8), :], srecv_sem.at[step]
+    def spread(step, lo, n, sem):
+        dst = qkv_recv.at[step, pl.ds(lo, n), c // 8, rows_of(c % 8), :]
         for o in OFFSETS:
             to = col_at(o, 1)
             pltpu.make_async_remote_copy(
-                src_ref=qkv_send.at[step, to],
+                src_ref=qkv_send.at[step, to, pl.ds(lo, n)],
                 dst_ref=dst,
                 send_sem=ssend_sem.at[step],
                 recv_sem=sem,
                 device_id={"col": to},
                 device_id_type=MESH,
             ).start()
-        pltpu.make_async_copy(qkv_send.at[step, c], dst, sem).start()
-
-    def ring_copy(step, kv, way, t, j, plane):
-        dst = kv_all[step][kv].at[pl.ds(2 * plane + j * (2 // J), 2 // J)]
-        src = qkv_recv.at[step, kv + 1, pl.ds(j * (2 // J), 2 // J)] if t == 0 else dst
+        pltpu.make_async_copy(qkv_send.at[step, c, pl.ds(lo, n)], dst, sem).start()
+
+    def z_copy(step, kv, origin, hop, j):
+        dst = kv_all[step][kv].at[2 * ((z - origin + NZ) % NZ) + j]
+        index = (origin + hop) % NZ
         return pltpu.make_async_remote_copy(
-            src_ref=src,
+            src_ref=dst if origin else qkv_recv.at[step, kv, j],
             dst_ref=dst,
-            send_sem=ring_send.at[step, kv, way, t, j],
-            recv_sem=ring_recv.at[step, kv, way, t, j],
-            device_id={"row": right if way == 0 else left},
+            send_sem=ring_send.at[step, kv, index, j],
+            recv_sem=ring_recv.at[step, kv, index, j],
+            device_id={"row": (z + hop + NZ) % NZ},
             device_id_type=MESH,
         )
 
-    def ring_plane(way, t):
-        return (z - t + NZ) % NZ if way == 0 else (z + t) % NZ
-
-    def ring_used(kv, way, t, j):
-        return t < 3 or (way == kv if J == 1 else (j < J // 2) == (way == 0))
-
-    def ring_turn(step, kv, t):
-        for j in range(J):
-            for way in range(2):
-                if not ring_used(kv, way, t, j):
-                    continue
-                if t > 0:
-                    ring_copy(step, kv, way, t - 1, j, ring_plane(way, t)).wait_recv()
-                ring_copy(step, kv, way, t, j, ring_plane(way, t)).start()
-
-    def ring_finish(step, kv):
-        for t in (2, 3):
-            for way in range(2):
-                for j in range(J):
-                    if ring_used(kv, way, t, j) and not (t == 2 and ring_used(kv, way, 3, j)):
-                        ring_copy(step, kv, way, t, j, ring_plane(way, t + 1)).wait_recv()
+    def z_wait(step, kv, come, j):
+        if (step, kv, come, j) not in waited:
+            waited.add((step, kv, come, j))
+            drain(kv_all[step][kv].at[2 * ((z - come + NZ) % NZ) + j], ring_recv.at[step, kv, come % NZ, j])
+
+    wt = wb_ref[...]
+
+    def chunk(ch, carry):
+        pair_copy(ch).wait()
+        for i in range(CH):
+            stage[i * HEADS : (i + 1) * HEADS, :] = lax.dot_general(
+                wt, pair_buf[ch * CH + i], NT, preferred_element_type=F32
+            )
+        for h in range(HEADS):
+            tile = stage[pl.ds(h, CH, stride=HEADS), :]
+            bias_send[h // 2, h % 2, pl.ds(pl.multiple_of(ch * CH, CH), CH), :] = tile.astype(BF)
+        return carry
 
     def make_bias():
-        wt = wb_ref[...]
-
-        def chunk(ch, carry):
-            pair_copy(ch).wait()
-            for i in range(CH):
-                stage[i * HEADS : (i + 1) * HEADS, :] = lax.dot_general(
-                    wt, pair_buf[ch * CH + i], NT, preferred_element_type=F32
-                )
-            for h in range(HEADS):
-                tile = stage[pl.ds(h, CH, stride=HEADS), :]
-                bias_send[h // 2, h % 2, pl.ds(pl.multiple_of(ch * CH, CH), CH), :] = tile.astype(BF)
-            return carry
+
+        def turn(to):
+            for hh in range(2):
+                bias_send[to, hh] = bias_send[to, hh].astype(F32).T.astype(BF)
 
         for g in range(PIECES):
-            lax.fori_loop(g * CHUNKS // PIECES, (g + 1) * CHUNKS // PIECES, chunk, 0)
+            lax.fori_loop(EARLY, CHUNKS, chunk, 0)
             part = pl.ds(g * BLK // PIECES, BLK // PIECES)
             for o in OFFSETS:
                 to = col_at(o, 1)
+                turn(to)
                 pltpu.make_async_remote_copy(
                     src_ref=bias_send.at[to, :, part, :],
                     dst_ref=bias_all.at[s, c, :, part, :],
@@ -166,6 +179,7 @@
                     device_id={"col": to},
                     device_id_type=MESH,
                 ).start()
+        turn(c)
         pltpu.make_async_copy(bias_send.at[c], bias_all.at[s, c], brecv_sem.at[c]).start()
 
     def pass_bias(col):
@@ -188,7 +202,7 @@
                 kb = slot_of(qb, slot)
                 at = jnp.maximum(kb, 0)
                 for hh in range(2):
-                    tile = jnp.where(kb >= 0, bias_all[qb, at, hh].astype(F32).T, F32(-1e30))
+                    tile = jnp.where(kb >= 0, bias_all[qb, at, hh].astype(F32), F32(-1e30))
                     kcat[qb, hh, slot * BLK : (slot + 1) * BLK, 128:] = tile.astype(BF)
 
     def block_of(step, kv, kb):
@@ -213,7 +227,7 @@
     def soften(step, lo, hi):
         def unit(it, carry):
             qb, hh = it // 2, it % 2
-            q = qkv_recv[step, 0, qb]
+            q = qkv_recv[step, 2, qb]
             rows = []
             for k in range(SAMP):
                 pick = (wide // HD == 2 * k + hh).astype(F32).astype(BF)
@@ -275,27 +289,29 @@
         out = jnp.dot(attn, wout_ref[...], preferred_element_type=F32)
         return x_ref[...] + out + 0.5 * 0.5**step * noise_ref[step]
 
-    x_ref[...] = state_ref[...]
+    for k in range(2):
+        loads[k].wait()
     vcat[:, :, 128:] = jnp.ones((2, KEYS, 128), BF)
     num[...] = jnp.zeros_like(num)
     den[...] = jnp.ones_like(den)
-    project(0)
-    pl.semaphore_wait(barrier, len(OFFSETS) + 3)
     for step in range(STEPS):
-        if step:
-            project(step)
-        spread(step)
+        project(step)
         if step == 0:
             make_bias()
-        drain(qkv_recv.at[step], srecv_sem.at[step])
-        ring_turn(step, 0, 0)
-        ring_turn(step, 1, 0)
         for kv in range(2):
-            kv_all[step][kv][pl.ds(2 * z, 2)] = qkv_recv[step, kv + 1]
-        for t in range(1, 4):
-            ring_turn(step, 0, t)
-            ring_turn(step, 1, t)
-        ring_finish(step, 0)
+            if kv == 0:
+                drain(qkv_recv.at[step, 0], krecv_sem.at[step])
+            else:
+                drain(qkv_recv.at[step, pl.ds(1, 2)], srecv_sem.at[step])
+            for origin, hop, j in FIRST:
+                z_copy(step, kv, origin, hop, j).start()
+            kv_all[step][kv][pl.ds(2 * z, 2)] = qkv_recv[step, kv]
+        for kv, origin, hop, j in LATER:
+            z_wait(step, kv, origin, j)
+            z_copy(step, kv, origin, hop, j).start()
+        for come in COMES:
+            for j in range(2):
+                z_wait(step, 0, come, j)
         place_keys(step)
         if step == 0:
             pass_bias(c)
@@ -304,10 +320,15 @@
             drain(bias_all.at[1 - s], frecv_sem)
             place_bias()
         soften(step, 0, 4)
-        ring_finish(step, 1)
+        for come in COMES:
+            for j in range(2):
+                z_wait(step, 1, come, j)
         place_values(step)
         mix(step)
         give_back(step)
+        if step == 0:
+            for k in (2, 3):
+                loads[k].wait()
         x = update(step)
         if step < STEPS - 1:
             x_ref[...] = x
@@ -319,26 +340,26 @@
     for step in range(STEPS):
         drain(qkv_send.at[step, pl.ds(0, NC - 1)], ssend_sem.at[step])
         drain(attn_send.at[step, pl.ds(0, (NC - 1) * ROWS), :], asend_sem.at[step])
-        for kv in range(2):
-            for way in range(2):
-                for t in range(4):
-                    for j in range(J):
-                        if ring_used(kv, way, t, j):
-                            ring_copy(step, kv, way, t, j, ring_plane(way, t)).wait_send()
+        for kv, origin, hop, j in tuple((kv, *f) for kv in range(2) for f in FIRST) + LATER:
+            z_copy(step, kv, origin, hop, j).wait_send()
 
 
 def body(state, noise, pair, contacts, norm_gain, w_qkv, w_out, w_bias):
     vmem = pl.BlockSpec(memory_space=pltpu.VMEM)
+    hbm = pl.BlockSpec(memory_space=pltpu.HBM)
     dma = pltpu.SemaphoreType.DMA
     out = pl.pallas_call(
         kernel,
         out_shape=jax.ShapeDtypeStruct((SAMP * ROWS, DS), F32),
         in_specs=[
-            vmem, vmem, pl.BlockSpec(memory_space=pltpu.HBM), pl.BlockSpec(memory_space=pltpu.SMEM),
-            vmem, vmem, vmem, vmem,
+            hbm, hbm, hbm, pl.BlockSpec(memory_space=pltpu.SMEM), vmem, hbm, hbm, vmem,
         ],
         out_specs=vmem,
         scratch_shapes=[
+            pltpu.VMEM((STEPS, SAMP * ROWS, DS), F32),
+            pltpu.VMEM((DS, 3 * DS), BF),
+            pltpu.VMEM((DS, DS), BF),
+            dma((4,)),
             pltpu.VMEM((SAMP * ROWS, DS), F32),
             pltpu.VMEM((BLK, BLK, CP), BF),
             pltpu.VMEM((CH * HEADS, BLK), F32),
@@ -365,8 +386,9 @@
             dma,
             dma((STEPS,)),
             dma((STEPS,)),
-            dma((STEPS, 2, 2, 4, J)),
-            dma((STEPS, 2, 2, 4, J)),
+            dma((STEPS,)),
+            dma((STEPS, 2, NZ, 2)),
+            dma((STEPS, 2, NZ, 2)),
             dma((STEPS,)),
             dma((STEPS,)),
         ],

time: 72.4 us -> 70.7 us (0.977)
  Pallas kernels: 70.7 us -> 68.9 us
    pallas_call x1, Pallas kernels: 70.7 us -> 68.9 us  [body(): pl.pallas_call(kernel, out_shape=jax.ShapeDtypeStruct((SAMP * ROWS, DS),...]
where the time goes in v3:
time: 70.7 us; the launch traced here: 70.4 us
  Pallas kernels  68.9 us (97%)
  local copies, waits for them, and re-layouts  1.57 us (2%)
    pallas_call x1, Pallas kernels, body(): pl.pallas_call(kernel, out_shape=jax.ShapeDtypeStruct((SAMP * ROWS, DS),...  68.9 us
    unnamed x1, local copies, waits for them, and re-layouts  1.57 us

profile of v3, /device:TPU:32, one launch (start us, length us, event | category | flops | bytes accessed | tf_op | source)
XLA Modules:
  0.0 70.4 jit_solution(16923071600009259000)
XLA Ops:
  0.0 68.9 %denoise.1 = f32[64,512]{1,0:T(8,128)} custom-call(f32[64,512]{1,0:T(8,128)} %bitcast.8, f32[2,64,512]{2,1,0:T(8,128)} %bitcast.7, bf16[256,128,128]{2,1,0:T(8,128)(2,1)} %pair_ref.1, s32[6,16]{1,0:T(8,128)} %bitcast.10, f32[1,512]{1,0:T(1,128)} %bitcast.11, bf16[512,1536]{1,0:T(8,128)(2,1)} %wqkv_hbm.1, bf16[512,512]{1,0:T(8,128)(2,1)} %wout_hbm.1, ...), custom_call_target="tpu_custom_call" | custom-call | tf_op jit(solution)/shard_map/denoise/pallas_call | solution.py:351
  68.9 1.6 %copy.10 = f32[4,16,512]{2,1,0:T(8,128)} copy(f32[4,16,512]{2,1,0:T(8,128)} %bitcast.6) | data formatting | bytes 262144

commit v4 on v3

--- a/solution.py
+++ b/solution.py
@@ -287,7 +287,8 @@
             [jnp.concatenate([columns[t][k] for t in range(4)], axis=1) for k in range(SAMP)], axis=0
         ).astype(BF)
         out = jnp.dot(attn, wout_ref[...], preferred_element_type=F32)
-        return x_ref[...] + out + 0.5 * 0.5**step * noise_ref[step]
+        out = x_ref[...] + out
+        return out + 0.5 * 0.5**step * noise_ref[step] if step < STEPS - 1 else out
 
     for k in range(2):
         loads[k].wait()
@@ -406,7 +407,7 @@
         w_out,
         w_bias.T,
     )
-    return out.reshape(SAMP, ROWS, DS)
+    return out.reshape(SAMP, ROWS, DS) + 0.5 * 0.5 ** (STEPS - 1) * noise[STEPS - 1]
 
 
 def solution(mesh):

time: 70.7 us -> 71 us (level)
  other arithmetic: 0 us -> 1.58 us
  local copies, waits for them, and re-layouts: 1.57 us -> 0.01 us
    add x0 -> x1, other arithmetic: none -> 1.58 us  [body(): out.reshape(SAMP, ROWS, DS) + 0.5 * 0.5 ** (STEPS - 1) * noise[STEPS - 1]]
    unnamed x1 -> x2, local copies, waits for them, and re-layouts: 1.57 us -> 0.01 us
where the time goes in v4:
time: 71 us; the launch traced here: 70.6 us
  Pallas kernels  69 us (97%)
  other arithmetic  1.58 us (2%)
    pallas_call x1, Pallas kernels, body(): pl.pallas_call(kernel, out_shape=jax.ShapeDtypeStruct((SAMP * ROWS, DS),...  69 us
    add x1, other arithmetic, body(): out.reshape(SAMP, ROWS, DS) + 0.5 * 0.5 ** (STEPS - 1) * noise[STEPS - 1]  1.58 us

profile of v4, /device:TPU:32, one launch (start us, length us, event | category | flops | bytes accessed | tf_op | source)
XLA Modules:
  0.0 70.6 jit_solution(3110613383844554013)
XLA Ops:
  0.0 0.0 copy-start
  0.0 69.0 %denoise.1 = f32[64,512]{1,0:T(8,128)} custom-call(f32[64,512]{1,0:T(8,128)} %bitcast.10, f32[2,64,512]{2,1,0:T(8,128)} %bitcast.8, bf16[256,128,128]{2,1,0:T(8,128)(2,1)} %pair_ref.1, s32[6,16]{1,0:T(8,128)} %bitcast.12, f32[1,512]{1,0:T(1,128)} %bitcast.13, bf16[512,1536]{1,0:T(8,128)(2,1)} %wqkv_hbm.1, bf16[512,512]{1,0:T(8,128)(2,1)} %wout_hbm.1, ...), custom_call_target="tpu_custom_call" | custom-call | tf_op jit(solution)/shard_map/denoise/pallas_call | solution.py:352
  69.0 0.0 copy-done
  69.0 1.6 %bitcast_add_fusion = f32[4,16,512]{2,1,0:T(8,128)} fusion(f32[4,16,512]{2,1,0:T(8,128)} %bitcast.9, f32[2,4,16,512]{3,2,1,0:T(8,128)S(1)} %copy-done), kind=kLoop, calls=%fused_computation | loop fusion | flops 65536 | bytes 393216 | tf_op jit(solution)/shard_map/add | solution.py:410
Async XLA Ops:
  0.0 69.0 %copy-start = (f32[2,4,16,512]{3,2,1,0:T(8,128)S(1)}, f32[2,4,16,512]{3,2,1,0:T(8,128)}, u32[]{:S(2)}) copy-start(f32[2,4,16,512]{3,2,1,0:T(8,128)} %param.9) | copy-start | bytes 786436
